TPU v7x, 512 devices: a whole 4x4x16 slice. The times are simulated.
512 devices in a mesh: tile: 128 (over z, y, core), fac: 4 (over x).
Axes of the slice: x: 4, y: 4, z: 16, core: 2. Of those that a mesh axis runs over, the one named last changes fastest.
Arguments:
- panel: float32 [64, 1024, 2048], P('fac', 'tile'), may hold values from -7000 to 7000
- materials: int32 [1024, 2048], P('tile'), may hold values from 0 to 7
- table: float32 [4, 8], replicated, may hold values from 0.2 to 5
- shifts: float32 [8], replicated, may hold values from 0.05 to 0.5
- shift_pick: int32 [1], replicated, may hold values from 0 to 7
Outputs:
- basis: float32 [64, 1024, 2048], P('fac', 'tile')
All inputs are finite; a program needn't handle non-finite values.
Results may differ from a plain program's by a relative error of at most 0.0003.
Values sent between devices are 32-bit elements; how exact they have to be, the bound alone decides.
A program may use at most 64 MiB of HBM per device.

v0:
```python
import jax
import jax.numpy as jnp
from jax import lax
from jax.sharding import PartitionSpec as P

NZ = 64
SWEEPS = 4
OMEGA = 0.8


def padded(value, sides, width):
    for axis, dim in sides:
        count, length = (lax.axis_size(axis), value.shape[dim])
        up = [(i, (i + 1) % count) for i in range(count - 1)]
        down = [(j, i) for i, j in up]
        last = lax.slice_in_dim(value, length - width, length, axis=dim)
        initial = lax.slice_in_dim(value, 0, width, axis=dim)
        before = lax.ppermute(last, axis, up)
        after = lax.ppermute(initial, axis, down)
        value = jnp.concatenate([before, value, after], axis=dim)
    return value


def swapped(value, axis, apart):
    return lax.ppermute(value, axis, [(i, i ^ 1 << apart) for i in range(lax.axis_size(axis))])


def harmonic(first, second):
    total = first + second
    safe = jnp.where(total > 0, total, 1.0)
    return 2.0 * first * second / safe


def material_fields(materials, table):
    fields = jnp.zeros((4,) + materials.shape, jnp.float32)
    for index in range(table.shape[1]):
        fields = fields + jnp.where(materials[None] == index, table[:, index][:, None, None], 0.0)
    return fields


def coefficients(fields, shift_value):
    cond_x = fields[0]
    faces_x = harmonic(cond_x[:-1], cond_x[1:])
    prev_x = faces_x[:-1]
    next_x = faces_x[1:]
    inner = fields[:, 1:-1]
    cond_y = inner[1]
    cond_z = inner[2]
    capacity = inner[3]
    count = cond_y.shape[0]
    width = cond_y.shape[1]
    zeros_y = jnp.zeros((count, NZ), jnp.float32)
    zeros_z = jnp.zeros((count, 1), jnp.float32)
    upper_y = jnp.concatenate([cond_y[:, NZ:], zeros_y], 1)
    next_y = harmonic(cond_y, upper_y)
    prev_y = jnp.concatenate([zeros_y, next_y[:, :-NZ]], 1)
    layer = jnp.arange(width) % NZ
    upper_z = jnp.concatenate([cond_z[:, 1:], zeros_z], 1)
    upper_z = jnp.where(layer[None] < NZ - 1, upper_z, 0.0)
    next_z = harmonic(cond_z, upper_z)
    prev_z = jnp.concatenate([zeros_z, next_z[:, :-1]], 1)
    diagonal = shift_value * capacity + prev_x + next_x + prev_y + next_y + prev_z + next_z
    inverse = jnp.where(capacity > 0, 1.0 / jnp.where(capacity > 0, diagonal, 1.0), 0.0)
    return (prev_x, next_x, prev_y, next_y, prev_z, next_z, inverse)


def relax(extended, source, coeffs):
    prev_x, next_x, prev_y, next_y, prev_z, next_z, inverse = coeffs
    center = extended[:, 1:-1]
    shape_y = center.shape[:-1] + (NZ,)
    shape_z = center.shape[:-1] + (1,)
    up_y = jnp.concatenate([center[..., NZ:], jnp.zeros(shape_y, center.dtype)], -1)
    down_y = jnp.concatenate([jnp.zeros(shape_y, center.dtype), center[..., :-NZ]], -1)
    up_z = jnp.concatenate([center[..., 1:], jnp.zeros(shape_z, center.dtype)], -1)
    down_z = jnp.concatenate([jnp.zeros(shape_z, center.dtype), center[..., :-1]], -1)
    beside = prev_x * extended[:, :-2] + next_x * extended[:, 2:]
    beside = beside + next_y * up_y + prev_y * down_y + next_z * up_z + prev_z * down_z
    return (1.0 - OMEGA) * center + OMEGA * (source + beside) * inverse


def gram_of(matrix):
    return jnp.dot(
        matrix, matrix.T, precision=lax.Precision.HIGHEST, preferred_element_type=jnp.float32
    )


def per_device(panel, materials, table, shifts, shift_pick):
    picker = jnp.arange(shifts.shape[0]) == shift_pick[0]
    shift_value = jnp.sum(jnp.where(picker, shifts, 0.0))
    fields = material_fields(materials, table)
    fields_ext = padded(fields, (("tile", 1),), 1)
    coeffs = coefficients(fields_ext, shift_value)
    solution = panel * coeffs[6][None]
    for sweep_index in range(SWEEPS):
        extended = padded(solution, (("tile", 1),), 1)
        solution = relax(extended, panel, coeffs)
    own_cols = solution.shape[0]
    column_count = 2 * own_cols
    ncells = solution.shape[1] * lax.axis_size("tile") * solution.shape[2]
    position = lax.axis_index("fac")
    half_id = position % 2
    half_rows = solution.shape[1] // 2
    keeping = lax.dynamic_slice_in_dim(solution, half_id * half_rows, half_rows, 1)
    giving = lax.dynamic_slice_in_dim(solution, (1 - half_id) * half_rows, half_rows, 1)
    received = swapped(giving, "fac", 0)
    merged = jnp.where(
        half_id == 0,
        jnp.concatenate([keeping, received], 0),
        jnp.concatenate([received, keeping], 0),
    )
    matrix = merged.reshape(column_count, -1)
    partial_value = gram_of(matrix)
    tile_sum = lax.psum(partial_value, "tile")
    total = tile_sum + swapped(tile_sum, "fac", 0)
    lower_factor = jnp.linalg.cholesky(total / ncells)
    ortho = lax.linalg.triangular_solve(lower_factor, matrix, left_side=True, lower=True).reshape(
        merged.shape
    )
    mine = lax.dynamic_slice_in_dim(ortho, half_id * own_cols, own_cols, 0)
    theirs = lax.dynamic_slice_in_dim(ortho, (1 - half_id) * own_cols, own_cols, 0)
    returned = swapped(theirs, "fac", 0)
    result = jnp.where(
        half_id == 0, jnp.concatenate([mine, returned], 1), jnp.concatenate([returned, mine], 1)
    )
    return result


def solution(mesh):
    placed = (P("fac", "tile", None), P("tile", None), P(), P(), P())
    return jax.shard_map(
        per_device, mesh=mesh, in_specs=placed, out_specs=P("fac", "tile", None), check_vma=False
    )
```

profile of v0, /device:TPU:262, one launch (start us, length us, event | category | flops | bytes accessed | tf_op | source)
XLA Modules:
  0.0 602.3 jit_solution(5284592554948806002)
XLA Ops:
  0.0 0.9 broadcast_compare_fusion.7
  0.9 0.0 copy-done.1
  0.9 0.3 slice_reduce_fusion.7
  1.2 0.3 select_add_fusion
  1.6 1.9 collective-permute-start
  3.5 7.0 %collective-permute-start.1 = (f32[4,1,2048]{2,1,0:T(1,128)S(1)}, f32[4,1,2048]{2,1,0:T(1,128)S(1)}, u32[]{:S(2)}, u32[]{:S(2)}) collective-permute-start(f32[4,1,2048]{2,1,0:T(1,128)S(1)} %get-tuple-element.44), channel_id=1, source_target_pairs={{4,0},{8,4},{12,8},{16,12},{20,16},{24,20},{28,24},{32,28},{36,32}... | collective-permute-start | bytes 98312 | tf_op jit(solution)/shard_map/ppermute | solution.py:19
  10.5 0.0 copy-start.2
  10.5 0.0 copy-start
  10.6 0.1 slice.249
  10.6 0.1 slice.252
  11.5 0.1 fusion.52
  11.5 0.6 fusion.69
  12.1 0.0 collective-permute-done
  12.1 0.0 collective-permute-done.1
  12.1 0.1 fusion.49
  12.2 0.7 broadcast_multiply_fusion
  12.9 0.6 copy_multiply_fusion
  13.5 0.4 fusion.81
  13.9 1.9 collective-permute-start.2
  15.8 7.0 %collective-permute-start.3 = (f32[16,1,2048]{2,0,1:T(8,128)S(1)}, f32[16,1,2048]{2,0,1:T(8,128)S(1)}, u32[]{:S(2)}, u32[]{:S(2)}) collective-permute-start(f32[16,1,2048]{2,0,1:T(8,128)S(1)} %get-tuple-element.42), channel_id=1, source_target_pairs={{4,0},{8,4},{12,8},{16,12},{20,16},{24,20},{28,24},{32,28},{36,32}... | collective-permute-start | bytes 393224 | tf_op jit(solution)/shard_map/ppermute | solution.py:19
  22.8 0.4 fusion.82
  23.2 0.3 collective-permute-done.2
  23.5 1.8 collective-permute-done.3
  25.3 1.6 fusion.41
  26.9 0.4 fusion.78
  27.3 1.9 collective-permute-start.4
  29.2 7.1 %collective-permute-start.5 = (f32[16,1,2048]{2,0,1:T(8,128)S(1)}, f32[16,1,2048]{2,0,1:T(8,128)S(1)}, u32[]{:S(2)}, u32[]{:S(2)}) collective-permute-start(f32[16,1,2048]{2,0,1:T(8,128)S(1)} %get-tuple-element.36), channel_id=1, source_target_pairs={{4,0},{8,4},{12,8},{16,12},{20,16},{24,20},{28,24},{32,28},{36,32}... | collective-permute-start | bytes 393224 | tf_op jit(solution)/shard_map/ppermute | solution.py:19
  36.3 0.4 fusion.79
  36.7 0.3 collective-permute-done.4
  37.0 1.8 collective-permute-done.5
  38.8 1.6 fusion.31
  40.5 0.4 fusion.75
  40.8 1.9 collective-permute-start.6
  42.8 7.1 %collective-permute-start.7 = (f32[16,1,2048]{2,0,1:T(8,128)S(1)}, f32[16,1,2048]{2,0,1:T(8,128)S(1)}, u32[]{:S(2)}, u32[]{:S(2)}) collective-permute-start(f32[16,1,2048]{2,0,1:T(8,128)S(1)} %get-tuple-element.30), channel_id=1, source_target_pairs={{4,0},{8,4},{12,8},{16,12},{20,16},{24,20},{28,24},{32,28},{36,32}... | collective-permute-start | bytes 393224 | tf_op jit(solution)/shard_map/ppermute | solution.py:19
  49.9 0.4 fusion.76
  50.2 0.3 collective-permute-done.6
  50.6 1.8 collective-permute-done.7
  52.4 1.6 fusion.21
  54.0 0.4 fusion.72
  54.4 1.9 collective-permute-start.8
  56.3 7.1 %collective-permute-start.9 = (f32[16,1,2048]{2,0,1:T(8,128)S(1)}, f32[16,1,2048]{2,0,1:T(8,128)S(1)}, u32[]{:S(2)}, u32[]{:S(2)}) collective-permute-start(f32[16,1,2048]{2,0,1:T(8,128)S(1)} %get-tuple-element.24), channel_id=1, source_target_pairs={{4,0},{8,4},{12,8},{16,12},{20,16},{24,20},{28,24},{32,28},{36,32}... | collective-permute-start | bytes 393224 | tf_op jit(solution)/shard_map/ppermute | solution.py:19
  63.4 0.4 fusion.73
  63.8 0.3 collective-permute-done.8
  64.1 1.8 collective-permute-done.9
  65.9 1.6 fusion.11
  67.5 0.1 constant_dynamic-slice_fusion.3
  67.6 2.9 collective-permute-start.10
  70.6 8.1 %collective-permute-done.10 = f32[16,4,2048]{2,0,1:T(8,128)S(1)} collective-permute-done((f32[16,4,2048]{2,0,1:T(8,128)S(1)}, f32[16,4,2048]{2,0,1:T(8,128)S(1)}, u32[]{:S(2)}, u32[]{:S(2)}) %collective-permute-start.10) | collective-permute-done | bytes 524320 | tf_op jit(solution)/shard_map/ppermute | solution.py:25
  78.7 1.0 convolution_bitcast_fusion
  79.7 496.3 %psum.7 = f32[32,32]{0,1:T(8,128)S(1)} all-reduce(f32[32,32]{0,1:T(8,128)S(1)} %convolution_bitcast_fusion), channel_id=1, replica_groups=mesh['tile'=128,'fac'=4] {'tile'}, use_global_device_ids=true, to_apply=%region_1.2 | all-reduce | flops 1024 | bytes 8192 | tf_op jit(solution)/shard_map/psum | solution.py:113
  576.0 2.7 collective-permute-start.11
  578.8 0.1 maximum_select_fusion.2
  578.9 2.8 collective-permute-done.11
  581.6 0.1 copy.25
  581.7 2.9 cholesky.16
  584.7 0.6 compare_reduce_fusion
  585.3 0.7 fusion.62
  586.0 2.4 custom-call.6
  588.4 1.1 fusion
  589.5 0.1 constant_dynamic-slice_fusion.1
  589.6 2.7 collective-permute-start.12
  592.3 8.3 %collective-permute-done.12 = f32[16,4,2048]{2,0,1:T(8,128)S(1)} collective-permute-done((f32[16,4,2048]{2,0,1:T(8,128)S(1)}, f32[16,4,2048]{2,0,1:T(8,128)S(1)}, u32[]{:S(2)}, u32[]{:S(2)}) %collective-permute-start.12) | collective-permute-done | bytes 524320 | tf_op jit(solution)/shard_map/ppermute | solution.py:25
  600.6 0.1 maximum_select_fusion.3
  600.7 1.6 copy.30
  (15 shorter events, 0.3 us)
Async XLA Ops:
  0.0 0.9 copy-start.1
  1.6 10.5 %collective-permute-start = (f32[4,1,2048]{2,1,0:T(1,128)S(1)}, f32[4,1,2048]{2,1,0:T(1,128)S(1)}, u32[]{:S(2)}, u32[]{:S(2)}) collective-permute-start(f32[4,1,2048]{2,1,0:T(1,128)S(1)} %get-tuple-element.43), channel_id=1, source_target_pairs={{0,4},{4,8},{8,12},{12,16},{16,20},{20,24},{24,28},{28,32},{32,36}... | collective-permute-start | bytes 98312 | tf_op jit(solution)/shard_map/ppermute | solution.py:18
  3.5 8.6 %collective-permute-start.1 = (f32[4,1,2048]{2,1,0:T(1,128)S(1)}, f32[4,1,2048]{2,1,0:T(1,128)S(1)}, u32[]{:S(2)}, u32[]{:S(2)}) collective-permute-start(f32[4,1,2048]{2,1,0:T(1,128)S(1)} %get-tuple-element.44), channel_id=1, source_target_pairs={{4,0},{8,4},{12,8},{16,12},{20,16},{24,20},{28,24},{32,28},{36,32}... | collective-permute-start | bytes 98312 | tf_op jit(solution)/shard_map/ppermute | solution.py:19
  10.5 1.0 copy-start.2
  10.5 2.4 copy-start
  13.9 9.6 %collective-permute-start.2 = (f32[16,1,2048]{2,0,1:T(8,128)S(1)}, f32[16,1,2048]{2,0,1:T(8,128)S(1)}, u32[]{:S(2)}, u32[]{:S(2)}) collective-permute-start(f32[16,1,2048]{2,0,1:T(8,128)S(1)} %get-tuple-element.41), channel_id=1, source_target_pairs={{0,4},{4,8},{8,12},{12,16},{16,20},{20,24},{24,28},{28,32},{32,36}... | collective-permute-start | bytes 393224 | tf_op jit(solution)/shard_map/ppermute | solution.py:18
  15.8 9.5 %collective-permute-start.3 = (f32[16,1,2048]{2,0,1:T(8,128)S(1)}, f32[16,1,2048]{2,0,1:T(8,128)S(1)}, u32[]{:S(2)}, u32[]{:S(2)}) collective-permute-start(f32[16,1,2048]{2,0,1:T(8,128)S(1)} %get-tuple-element.42), channel_id=1, source_target_pairs={{4,0},{8,4},{12,8},{16,12},{20,16},{24,20},{28,24},{32,28},{36,32}... | collective-permute-start | bytes 393224 | tf_op jit(solution)/shard_map/ppermute | solution.py:19
  27.3 9.7 %collective-permute-start.4 = (f32[16,1,2048]{2,0,1:T(8,128)S(1)}, f32[16,1,2048]{2,0,1:T(8,128)S(1)}, u32[]{:S(2)}, u32[]{:S(2)}) collective-permute-start(f32[16,1,2048]{2,0,1:T(8,128)S(1)} %get-tuple-element.35), channel_id=1, source_target_pairs={{0,4},{4,8},{8,12},{12,16},{16,20},{20,24},{24,28},{28,32},{32,36}... | collective-permute-start | bytes 393224 | tf_op jit(solution)/shard_map/ppermute | solution.py:18
  29.2 9.6 %collective-permute-start.5 = (f32[16,1,2048]{2,0,1:T(8,128)S(1)}, f32[16,1,2048]{2,0,1:T(8,128)S(1)}, u32[]{:S(2)}, u32[]{:S(2)}) collective-permute-start(f32[16,1,2048]{2,0,1:T(8,128)S(1)} %get-tuple-element.36), channel_id=1, source_target_pairs={{4,0},{8,4},{12,8},{16,12},{20,16},{24,20},{28,24},{32,28},{36,32}... | collective-permute-start | bytes 393224 | tf_op jit(solution)/shard_map/ppermute | solution.py:19
  40.8 9.7 %collective-permute-start.6 = (f32[16,1,2048]{2,0,1:T(8,128)S(1)}, f32[16,1,2048]{2,0,1:T(8,128)S(1)}, u32[]{:S(2)}, u32[]{:S(2)}) collective-permute-start(f32[16,1,2048]{2,0,1:T(8,128)S(1)} %get-tuple-element.29), channel_id=1, source_target_pairs={{0,4},{4,8},{8,12},{12,16},{16,20},{20,24},{24,28},{28,32},{32,36}... | collective-permute-start | bytes 393224 | tf_op jit(solution)/shard_map/ppermute | solution.py:18
  42.8 9.6 %collective-permute-start.7 = (f32[16,1,2048]{2,0,1:T(8,128)S(1)}, f32[16,1,2048]{2,0,1:T(8,128)S(1)}, u32[]{:S(2)}, u32[]{:S(2)}) collective-permute-start(f32[16,1,2048]{2,0,1:T(8,128)S(1)} %get-tuple-element.30), channel_id=1, source_target_pairs={{4,0},{8,4},{12,8},{16,12},{20,16},{24,20},{28,24},{32,28},{36,32}... | collective-permute-start | bytes 393224 | tf_op jit(solution)/shard_map/ppermute | solution.py:19
  54.4 9.7 %collective-permute-start.8 = (f32[16,1,2048]{2,0,1:T(8,128)S(1)}, f32[16,1,2048]{2,0,1:T(8,128)S(1)}, u32[]{:S(2)}, u32[]{:S(2)}) collective-permute-start(f32[16,1,2048]{2,0,1:T(8,128)S(1)} %get-tuple-element.23), channel_id=1, source_target_pairs={{0,4},{4,8},{8,12},{12,16},{16,20},{20,24},{24,28},{28,32},{32,36}... | collective-permute-start | bytes 393224 | tf_op jit(solution)/shard_map/ppermute | solution.py:18
  56.3 9.6 %collective-permute-start.9 = (f32[16,1,2048]{2,0,1:T(8,128)S(1)}, f32[16,1,2048]{2,0,1:T(8,128)S(1)}, u32[]{:S(2)}, u32[]{:S(2)}) collective-permute-start(f32[16,1,2048]{2,0,1:T(8,128)S(1)} %get-tuple-element.24), channel_id=1, source_target_pairs={{4,0},{8,4},{12,8},{16,12},{20,16},{24,20},{28,24},{32,28},{36,32}... | collective-permute-start | bytes 393224 | tf_op jit(solution)/shard_map/ppermute | solution.py:19
  67.6 11.1 %collective-permute-start.10 = (f32[16,4,2048]{2,0,1:T(8,128)S(1)}, f32[16,4,2048]{2,0,1:T(8,128)S(1)}, u32[]{:S(2)}, u32[]{:S(2)}) collective-permute-start(f32[16,4,2048]{2,0,1:T(8,128)S(1)} %get-tuple-element.18), channel_id=1, source_target_pairs={{0,1},{1,0},{2,3},{3,2},{4,5},{5,4},{6,7},{7,6},{8,9},{9,8},{10,11... | collective-permute-start | bytes 1572872 | tf_op jit(solution)/shard_map/ppermute | solution.py:25
  576.0 5.6 collective-permute-start.11
  589.6 11.1 %collective-permute-start.12 = (f32[16,4,2048]{2,0,1:T(8,128)S(1)}, f32[16,4,2048]{2,0,1:T(8,128)S(1)}, u32[]{:S(2)}, u32[]{:S(2)}) collective-permute-start(f32[16,4,2048]{2,0,1:T(8,128)S(1)} %get-tuple-element.16), channel_id=1, source_target_pairs={{0,1},{1,0},{2,3},{3,2},{4,5},{5,4},{6,7},{7,6},{8,9},{9,8},{10,11... | collective-permute-start | bytes 1572872 | tf_op jit(solution)/shard_map/ppermute | solution.py:25
where the time goes:
time: 603 us; the launch traced here: 602 us
  blocking collectives  496 us (82%)
  starting transfers between devices  53.2 us (9%)
  waiting for transfers between devices  27.7 us (5%)
  other arithmetic  16.6 us (3%)
    psum x1, blocking collectives, per_device(): tile_sum = lax.psum(partial_value, 'tile')  496 us
    ppermute x5, starting transfers between devices, padded(): after = lax.ppermute(initial, axis, down)  35.2 us
    ppermute x3, waiting for transfers between devices, swapped(): lax.ppermute(value, axis, [(i, i ^ 1 << apart) for i in range(lax.axis_si...  19.2 us
  transfers between devices with their start and end apart: 13, of which 11 were waited for; matrix products, arithmetic and copies ran while one was open for 0% of the time, Pallas kernels for 0%

commit v1 on v0

--- a/solution.py
+++ b/solution.py
@@ -110,7 +110,7 @@
     )
     matrix = merged.reshape(column_count, -1)
     partial_value = gram_of(matrix)
-    tile_sum = lax.psum(partial_value, "tile")
+    tile_sum = jnp.sum(lax.all_gather(partial_value, "tile"), axis=0)
     total = tile_sum + swapped(tile_sum, "fac", 0)
     lower_factor = jnp.linalg.cholesky(total / ncells)
     ortho = lax.linalg.triangular_solve(lower_factor, matrix, left_side=True, lower=True).reshape(

time: 603 us -> 220 us (0.36)
  the two profiles are of different devices: /device:TPU:262 before, /device:TPU:2 now
where the time goes in v1:
time: 220 us; the launch traced here: 219 us
  blocking collectives  124 us (56%)
  starting transfers between devices  37.4 us (17%)
  waiting for transfers between devices  31.2 us (14%)
  other arithmetic  17.7 us (8%)
  local copies, waits for them, and re-layouts  6.37 us (3%)
    all_gather x1, blocking collectives, per_device(): tile_sum = jnp.sum(lax.all_gather(partial_value, 'tile'), axis=0)  124 us
    ppermute x3, waiting for transfers between devices, swapped(): lax.ppermute(value, axis, [(i, i ^ 1 << apart) for i in range(lax.axis_si...  23.8 us
    ppermute x5, starting transfers between devices, padded(): before = lax.ppermute(last, axis, up)  22.6 us
    ppermute x3, starting transfers between devices, swapped(): lax.ppermute(value, axis, [(i, i ^ 1 << apart) for i in range(lax.axis_si...  8.34 us
    ppermute x5, waiting for transfers between devices, padded(): after = lax.ppermute(initial, axis, down)  7.38 us
    add x4, other arithmetic, relax(): return (1.0 - OMEGA) * center + OMEGA * (source + beside) * inverse  6.47 us
    ppermute x5, starting transfers between devices, padded(): after = lax.ppermute(initial, axis, down)  6.46 us
  transfers between devices with their start and end apart: 13, of which 8 were waited for; matrix products, arithmetic and copies ran while one was open for 1% of the time, Pallas kernels for 0%

profile of v1, /device:TPU:2, one launch (start us, length us, event | category | flops | bytes accessed | tf_op | source)
XLA Modules:
  0.0 219.3 jit_solution(12313142447515671510)
XLA Ops:
  0.0 1.0 broadcast_compare_fusion.7
  1.0 1.3 slice_reduce_fusion.7
  2.3 0.3 select_add_fusion
  2.6 1.7 collective-permute-start
  4.4 1.3 collective-permute-start.1
  5.7 0.1 slice.249
  5.8 0.1 slice.252
  6.6 0.1 fusion.52
  6.6 1.3 fusion.69
  8.0 0.0 collective-permute-done
  8.0 0.9 collective-permute-done.1
  8.9 0.1 fusion.49
  8.9 0.8 broadcast_multiply_fusion
  9.7 0.0 copy-done
  9.7 0.6 copy_multiply_fusion
  10.4 0.4 fusion.81
  10.7 4.5 %collective-permute-start.2 = (f32[16,1,2048]{2,0,1:T(8,128)S(1)}, f32[16,1,2048]{2,0,1:T(8,128)S(1)}, u32[]{:S(2)}, u32[]{:S(2)}) collective-permute-start(f32[16,1,2048]{2,0,1:T(8,128)S(1)} %get-tuple-element.41), channel_id=1, source_target_pairs={{0,4},{4,8},{8,12},{12,16},{16,20},{20,24},{24,28},{28,32},{32,36}... | collective-permute-start | bytes 393224 | tf_op jit(solution)/shard_map/ppermute | solution.py:18
  15.3 1.3 collective-permute-start.3
  16.6 0.4 fusion.82
  17.0 0.0 collective-permute-done.2
  17.0 1.8 collective-permute-done.3
  18.7 1.6 fusion.41
  20.3 0.4 fusion.78
  20.7 5.5 %collective-permute-start.4 = (f32[16,1,2048]{2,0,1:T(8,128)S(1)}, f32[16,1,2048]{2,0,1:T(8,128)S(1)}, u32[]{:S(2)}, u32[]{:S(2)}) collective-permute-start(f32[16,1,2048]{2,0,1:T(8,128)S(1)} %get-tuple-element.35), channel_id=1, source_target_pairs={{0,4},{4,8},{8,12},{12,16},{16,20},{20,24},{24,28},{28,32},{32,36}... | collective-permute-start | bytes 393224 | tf_op jit(solution)/shard_map/ppermute | solution.py:18
  26.2 1.3 collective-permute-start.5
  27.5 0.4 fusion.79
  27.9 0.0 collective-permute-done.4
  27.9 1.6 collective-permute-done.5
  29.4 1.6 fusion.31
  31.1 0.4 fusion.75
  31.4 5.0 %collective-permute-start.6 = (f32[16,1,2048]{2,0,1:T(8,128)S(1)}, f32[16,1,2048]{2,0,1:T(8,128)S(1)}, u32[]{:S(2)}, u32[]{:S(2)}) collective-permute-start(f32[16,1,2048]{2,0,1:T(8,128)S(1)} %get-tuple-element.29), channel_id=1, source_target_pairs={{0,4},{4,8},{8,12},{12,16},{16,20},{20,24},{24,28},{28,32},{32,36}... | collective-permute-start | bytes 393224 | tf_op jit(solution)/shard_map/ppermute | solution.py:18
  36.4 1.3 collective-permute-start.7
  37.7 0.4 fusion.76
  38.1 0.0 collective-permute-done.6
  38.1 1.6 collective-permute-done.7
  39.7 1.6 fusion.21
  41.3 0.4 fusion.72
  41.7 5.9 %collective-permute-start.8 = (f32[16,1,2048]{2,0,1:T(8,128)S(1)}, f32[16,1,2048]{2,0,1:T(8,128)S(1)}, u32[]{:S(2)}, u32[]{:S(2)}) collective-permute-start(f32[16,1,2048]{2,0,1:T(8,128)S(1)} %get-tuple-element.23), channel_id=1, source_target_pairs={{0,4},{4,8},{8,12},{12,16},{16,20},{20,24},{24,28},{28,32},{32,36}... | collective-permute-start | bytes 393224 | tf_op jit(solution)/shard_map/ppermute | solution.py:18
  47.6 1.3 collective-permute-start.9
  48.9 0.4 fusion.73
  49.3 0.0 collective-permute-done.8
  49.3 1.6 collective-permute-done.9
  50.9 1.6 fusion.11
  52.5 0.1 constant_dynamic-slice_fusion.3
  52.6 3.5 %collective-permute-start.10 = (f32[16,4,2048]{2,0,1:T(8,128)S(1)}, f32[16,4,2048]{2,0,1:T(8,128)S(1)}, u32[]{:S(2)}, u32[]{:S(2)}) collective-permute-start(f32[16,4,2048]{2,0,1:T(8,128)S(1)} %get-tuple-element.18), channel_id=1, source_target_pairs={{0,1},{1,0},{2,3},{3,2},{4,5},{5,4},{6,7},{7,6},{8,9},{9,8},{10,11... | collective-permute-start | bytes 1572872 | tf_op jit(solution)/shard_map/ppermute | solution.py:25
  56.1 8.3 %collective-permute-done.10 = f32[16,4,2048]{2,0,1:T(8,128)S(1)} collective-permute-done((f32[16,4,2048]{2,0,1:T(8,128)S(1)}, f32[16,4,2048]{2,0,1:T(8,128)S(1)}, u32[]{:S(2)}, u32[]{:S(2)}) %collective-permute-start.10) | collective-permute-done | bytes 524320 | tf_op jit(solution)/shard_map/ppermute | solution.py:25
  64.4 1.0 convolution_bitcast_fusion
  65.3 123.5 %all-gather = f32[4096,32]{1,0:T(8,128)S(1)} all-gather(f32[32,32]{1,0:T(8,128)S(1)} %convolution_bitcast_fusion), channel_id=2, replica_groups=mesh['tile'=128,'fac'=4] {'tile'}, dimensions={0}, use_global_device_ids=true | all-gather | bytes 528384 | tf_op jit(solution)/shard_map/all_gather | solution.py:113
  188.9 0.2 reduce_sum.19
  189.1 0.1 copy.23
  189.1 2.4 %collective-permute-start.11 = (f32[32,32]{0,1:T(8,128)S(1)}, f32[32,32]{0,1:T(8,128)S(1)}, u32[]{:S(2)}, u32[]{:S(2)}) collective-permute-start(f32[32,32]{0,1:T(8,128)S(1)} %copy.23), channel_id=1, source_target_pairs={{0,1},{1,0},{2,3},{3,2},{4,5},{5,4},{6,7},{7,6},{8,9},{9,8},{10,11... | collective-permute-start | bytes 12296 | tf_op jit(solution)/shard_map/ppermute | solution.py:25
  191.6 0.1 maximum_select_fusion.2
  191.7 3.1 %collective-permute-done.11 = f32[32,32]{0,1:T(8,128)S(1)} collective-permute-done((f32[32,32]{0,1:T(8,128)S(1)}, f32[32,32]{0,1:T(8,128)S(1)}, u32[]{:S(2)}, u32[]{:S(2)}) %collective-permute-start.11) | collective-permute-done | bytes 4128 | tf_op jit(solution)/shard_map/ppermute | solution.py:25
  194.8 0.1 copy.24
  194.8 2.9 %cholesky.16 = f32[32,32]{1,0:T(8,128)S(1)} custom-call(f32[32,32]{1,0:T(8,128)S(1)} %fusion.64), custom_call_target="Cholesky" | custom-call | tf_op jit(solution)/shard_map/jit(cholesky)/cholesky | solution.py:115
  197.8 0.6 compare_reduce_fusion
  198.4 0.7 fusion.62
  199.1 2.4 %custom-call.6 = f32[1,32,32]{1,2,0:T(8,128)S(1)} custom-call(f32[1,32,32]{2,1,0:T(8,128)S(1)} %fusion.62), custom_call_target="InvertDiagBlocksLowerTriangular" | custom-call | tf_op jit(solution)/shard_map/triangular_solve | solution.py:116
  201.5 1.1 fusion
  202.6 0.1 constant_dynamic-slice_fusion.1
  202.7 2.4 %collective-permute-start.12 = (f32[16,4,2048]{2,0,1:T(8,128)S(1)}, f32[16,4,2048]{2,0,1:T(8,128)S(1)}, u32[]{:S(2)}, u32[]{:S(2)}) collective-permute-start(f32[16,4,2048]{2,0,1:T(8,128)S(1)} %get-tuple-element.16), channel_id=1, source_target_pairs={{0,1},{1,0},{2,3},{3,2},{4,5},{5,4},{6,7},{7,6},{8,9},{9,8},{10,11... | collective-permute-start | bytes 1572872 | tf_op jit(solution)/shard_map/ppermute | solution.py:25
  205.1 12.5 %collective-permute-done.12 = f32[16,4,2048]{2,0,1:T(8,128)S(1)} collective-permute-done((f32[16,4,2048]{2,0,1:T(8,128)S(1)}, f32[16,4,2048]{2,0,1:T(8,128)S(1)}, u32[]{:S(2)}, u32[]{:S(2)}) %collective-permute-start.12) | collective-permute-done | bytes 524320 | tf_op jit(solution)/shard_map/ppermute | solution.py:25
  217.6 0.1 maximum_select_fusion.3
  217.7 1.6 copy.29
  (13 shorter events, 0.3 us)
Async XLA Ops:
  0.0 9.7 %copy-start = (f32[16,8,2048]{2,1,0:T(8,128)S(1)}, f32[16,8,2048]{2,1,0:T(8,128)}, u32[]{:S(2)}) copy-start(f32[16,8,2048]{2,1,0:T(8,128)} %param.5) | copy-start | bytes 3145732
  2.6 5.3 %collective-permute-start = (f32[4,1,2048]{2,1,0:T(1,128)S(1)}, f32[4,1,2048]{2,1,0:T(1,128)S(1)}, u32[]{:S(2)}, u32[]{:S(2)}) collective-permute-start(f32[4,1,2048]{2,1,0:T(1,128)S(1)} %get-tuple-element.43), channel_id=1, source_target_pairs={{0,4},{4,8},{8,12},{12,16},{16,20},{20,24},{24,28},{28,32},{32,36}... | collective-permute-start | bytes 98312 | tf_op jit(solution)/shard_map/ppermute | solution.py:18
  4.4 4.5 %collective-permute-start.1 = (f32[4,1,2048]{2,1,0:T(1,128)S(1)}, f32[4,1,2048]{2,1,0:T(1,128)S(1)}, u32[]{:S(2)}, u32[]{:S(2)}) collective-permute-start(f32[4,1,2048]{2,1,0:T(1,128)S(1)} %get-tuple-element.44), channel_id=1, source_target_pairs={{4,0},{8,4},{12,8},{16,12},{20,16},{24,20},{28,24},{32,28},{36,32}... | collective-permute-start | bytes 98312 | tf_op jit(solution)/shard_map/ppermute | solution.py:19
  10.7 6.2 %collective-permute-start.2 = (f32[16,1,2048]{2,0,1:T(8,128)S(1)}, f32[16,1,2048]{2,0,1:T(8,128)S(1)}, u32[]{:S(2)}, u32[]{:S(2)}) collective-permute-start(f32[16,1,2048]{2,0,1:T(8,128)S(1)} %get-tuple-element.41), channel_id=1, source_target_pairs={{0,4},{4,8},{8,12},{12,16},{16,20},{20,24},{24,28},{28,32},{32,36}... | collective-permute-start | bytes 393224 | tf_op jit(solution)/shard_map/ppermute | solution.py:18
  15.3 3.4 %collective-permute-start.3 = (f32[16,1,2048]{2,0,1:T(8,128)S(1)}, f32[16,1,2048]{2,0,1:T(8,128)S(1)}, u32[]{:S(2)}, u32[]{:S(2)}) collective-permute-start(f32[16,1,2048]{2,0,1:T(8,128)S(1)} %get-tuple-element.42), channel_id=1, source_target_pairs={{4,0},{8,4},{12,8},{16,12},{20,16},{24,20},{28,24},{32,28},{36,32}... | collective-permute-start | bytes 393224 | tf_op jit(solution)/shard_map/ppermute | solution.py:19
  20.7 7.1 %collective-permute-start.4 = (f32[16,1,2048]{2,0,1:T(8,128)S(1)}, f32[16,1,2048]{2,0,1:T(8,128)S(1)}, u32[]{:S(2)}, u32[]{:S(2)}) collective-permute-start(f32[16,1,2048]{2,0,1:T(8,128)S(1)} %get-tuple-element.35), channel_id=1, source_target_pairs={{0,4},{4,8},{8,12},{12,16},{16,20},{20,24},{24,28},{28,32},{32,36}... | collective-permute-start | bytes 393224 | tf_op jit(solution)/shard_map/ppermute | solution.py:18
  26.2 3.2 %collective-permute-start.5 = (f32[16,1,2048]{2,0,1:T(8,128)S(1)}, f32[16,1,2048]{2,0,1:T(8,128)S(1)}, u32[]{:S(2)}, u32[]{:S(2)}) collective-permute-start(f32[16,1,2048]{2,0,1:T(8,128)S(1)} %get-tuple-element.36), channel_id=1, source_target_pairs={{4,0},{8,4},{12,8},{16,12},{20,16},{24,20},{28,24},{32,28},{36,32}... | collective-permute-start | bytes 393224 | tf_op jit(solution)/shard_map/ppermute | solution.py:19
  31.4 6.6 %collective-permute-start.6 = (f32[16,1,2048]{2,0,1:T(8,128)S(1)}, f32[16,1,2048]{2,0,1:T(8,128)S(1)}, u32[]{:S(2)}, u32[]{:S(2)}) collective-permute-start(f32[16,1,2048]{2,0,1:T(8,128)S(1)} %get-tuple-element.29), channel_id=1, source_target_pairs={{0,4},{4,8},{8,12},{12,16},{16,20},{20,24},{24,28},{28,32},{32,36}... | collective-permute-start | bytes 393224 | tf_op jit(solution)/shard_map/ppermute | solution.py:18
  36.4 3.2 %collective-permute-start.7 = (f32[16,1,2048]{2,0,1:T(8,128)S(1)}, f32[16,1,2048]{2,0,1:T(8,128)S(1)}, u32[]{:S(2)}, u32[]{:S(2)}) collective-permute-start(f32[16,1,2048]{2,0,1:T(8,128)S(1)} %get-tuple-element.30), channel_id=1, source_target_pairs={{4,0},{8,4},{12,8},{16,12},{20,16},{24,20},{28,24},{32,28},{36,32}... | collective-permute-start | bytes 393224 | tf_op jit(solution)/shard_map/ppermute | solution.py:19
  41.7 7.6 %collective-permute-start.8 = (f32[16,1,2048]{2,0,1:T(8,128)S(1)}, f32[16,1,2048]{2,0,1:T(8,128)S(1)}, u32[]{:S(2)}, u32[]{:S(2)}) collective-permute-start(f32[16,1,2048]{2,0,1:T(8,128)S(1)} %get-tuple-element.23), channel_id=1, source_target_pairs={{0,4},{4,8},{8,12},{12,16},{16,20},{20,24},{24,28},{28,32},{32,36}... | collective-permute-start | bytes 393224 | tf_op jit(solution)/shard_map/ppermute | solution.py:18
  47.6 3.2 %collective-permute-start.9 = (f32[16,1,2048]{2,0,1:T(8,128)S(1)}, f32[16,1,2048]{2,0,1:T(8,128)S(1)}, u32[]{:S(2)}, u32[]{:S(2)}) collective-permute-start(f32[16,1,2048]{2,0,1:T(8,128)S(1)} %get-tuple-element.24), channel_id=1, source_target_pairs={{4,0},{8,4},{12,8},{16,12},{20,16},{24,20},{28,24},{32,28},{36,32}... | collective-permute-start | bytes 393224 | tf_op jit(solution)/shard_map/ppermute | solution.py:19
  52.6 11.8 %collective-permute-start.10 = (f32[16,4,2048]{2,0,1:T(8,128)S(1)}, f32[16,4,2048]{2,0,1:T(8,128)S(1)}, u32[]{:S(2)}, u32[]{:S(2)}) collective-permute-start(f32[16,4,2048]{2,0,1:T(8,128)S(1)} %get-tuple-element.18), channel_id=1, source_target_pairs={{0,1},{1,0},{2,3},{3,2},{4,5},{5,4},{6,7},{7,6},{8,9},{9,8},{10,11... | collective-permute-start | bytes 1572872 | tf_op jit(solution)/shard_map/ppermute | solution.py:25
  189.1 5.6 %collective-permute-start.11 = (f32[32,32]{0,1:T(8,128)S(1)}, f32[32,32]{0,1:T(8,128)S(1)}, u32[]{:S(2)}, u32[]{:S(2)}) collective-permute-start(f32[32,32]{0,1:T(8,128)S(1)} %copy.23), channel_id=1, source_target_pairs={{0,1},{1,0},{2,3},{3,2},{4,5},{5,4},{6,7},{7,6},{8,9},{9,8},{10,11... | collective-permute-start | bytes 12296 | tf_op jit(solution)/shard_map/ppermute | solution.py:25
  202.7 14.9 %collective-permute-start.12 = (f32[16,4,2048]{2,0,1:T(8,128)S(1)}, f32[16,4,2048]{2,0,1:T(8,128)S(1)}, u32[]{:S(2)}, u32[]{:S(2)}) collective-permute-start(f32[16,4,2048]{2,0,1:T(8,128)S(1)} %get-tuple-element.16), channel_id=1, source_target_pairs={{0,1},{1,0},{2,3},{3,2},{4,5},{5,4},{6,7},{7,6},{8,9},{9,8},{10,11... | collective-permute-start | bytes 1572872 | tf_op jit(solution)/shard_map/ppermute | solution.py:25
